TPU v7x, 32 devices: a whole 2x2x4 slice. The times are simulated.
32 devices in a mesh: row: 4 (over z), col: 8 (over y, x, core).
Axes of the slice: x: 2, y: 2, z: 4, core: 2. Of those that a mesh axis runs over, the one named last changes fastest.
Arguments:
- positions: float32 [3, 65536], P(None, ('row', 'col')), may hold values from 0 to 1
- masses: float32 [1, 65536], P(None, ('row', 'col')), may hold values from 2e-09 to 2e-08
- counts: int32 [1, 512], P(None, ('row', 'col')), may hold values from 32 to 128
- sources: int32 [512, 8], P(('row', 'col')), may hold values from 0 to 47, as said below
Outputs:
- accel: float32 [3, 65536], P(None, ('row', 'col'))
Inputs may be any that keep to these rules, and one draw needn't show every extreme that they name: `sources`: each device's source ids name exactly 4 distinct leaves of the lower row neighbour and exactly 4 of the upper one.
All inputs are finite; a program needn't handle non-finite values.
Results may differ from a plain program's by a relative error of at most 0.00024.
Values sent between devices are 32-bit elements; how exact they have to be, the bound alone decides.
A program may use at most 64 MiB of HBM per device.

v0:
```python
import jax
import jax.numpy as jnp
from jax import lax
from jax.sharding import PartitionSpec as P

softening = 2.5e-07


def padded_2(shard, sides, width):
    for axis, dim in sides:
        size, length = (lax.axis_size(axis), shard.shape[dim])
        up = [(i, (i + 1) % size) for i in range(size)]
        down = [(j, i) for i, j in up]
        last = lax.slice_in_dim(shard, length - width, length, axis=dim)
        leading = lax.slice_in_dim(shard, 0, width, axis=dim)
        before = lax.ppermute(last, axis, up)
        after = lax.ppermute(leading, axis, down)
        shard = jnp.concatenate([before, shard, after], axis=dim)
    return shard


def leaf_forces(full_table, targets, sources, alive):
    count = targets.shape[0]
    width = targets.shape[2]
    target_groups = targets.reshape(count // 8, 8, 4, width)
    source_groups = sources.reshape(count // 8, 8, sources.shape[1])
    alive_groups = alive.reshape(count // 8, 8, width)

    def one_group(items):
        target, index, living = items
        source = full_table[index]
        delta_x = source[:, :, 0, None, :] - target[:, None, 0, :, None]
        delta_y = source[:, :, 1, None, :] - target[:, None, 1, :, None]
        delta_z = source[:, :, 2, None, :] - target[:, None, 2, :, None]
        spread = softening + delta_x * delta_x + delta_y * delta_y + delta_z * delta_z
        weight = source[:, :, 3, None, :] / (spread * jnp.sqrt(spread))
        pull_x = jnp.sum(weight * delta_x, axis=(1, 3))
        pull_y = jnp.sum(weight * delta_y, axis=(1, 3))
        pull_z = jnp.sum(weight * delta_z, axis=(1, 3))
        return jnp.stack([pull_x, pull_y, pull_z], axis=1) * living[:, None, :]

    out = lax.map(one_group, (target_groups, source_groups, alive_groups))
    return out.reshape(count, 3, width)


def on_device(positions, masses, counts, sources):
    coords, weights, livecount = (
        lax.all_to_all(positions, "col", split_axis=1, concat_axis=1, tiled=True),
        lax.all_to_all(masses, "col", split_axis=1, concat_axis=1, tiled=True),
        lax.all_to_all(counts, "col", split_axis=1, concat_axis=1, tiled=True),
    )
    leaves = livecount.shape[1]
    width = coords.shape[1] // leaves
    alive = (
        lax.broadcasted_iota(jnp.int32, (leaves, width), 1) < livecount.reshape(leaves, 1)
    ).astype(jnp.float32)
    table = jnp.concatenate(
        [coords.reshape(3, leaves, width), (weights.reshape(leaves, width) * alive)[None]], axis=0
    )
    table = table.transpose(1, 0, 2)
    padded = padded_2(table, (("row", 0),), leaves)
    full = jnp.concatenate(
        [padded[leaves : 2 * leaves], padded[:leaves], padded[2 * leaves :]], axis=0
    )
    result = leaf_forces(full, table, sources, alive)
    return result.transpose(1, 0, 2).reshape(3, leaves * width)


def solution(mesh):
    return jax.shard_map(
        on_device,
        mesh=mesh,
        in_specs=(
            P(None, ("row", "col")),
            P(None, ("row", "col")),
            P(None, ("row", "col")),
            P(("row", "col"), None),
        ),
        out_specs=P(None, ("row", "col")),
        check_vma=False,
    )
```

profile of v0, /device:TPU:0, one launch (start us, length us, event | category | flops | bytes accessed | tf_op | source)
XLA Modules:
  0.0 44.4 jit_solution(10030716377979728203)
XLA Ops:
  0.0 0.6 %broadcast.80 = s32[]{:T(128)} broadcast(s32[]{:T(128)} %copy.43), dimensions={} | broadcast | bytes 8 | tf_op args[2]
  0.6 1.4 %reduce.8 = s32[16]{0:T(128)S(1)} reduce(s32[1,16]{1,0:T(1,128)} %param.8, s32[]{:T(128)} %broadcast.80), dimensions={0}, to_apply=%param.8.reduce_sub_computation.3 | reduce | bytes 132 | tf_op args[2]
  2.0 0.1 all_to_all.20
  2.0 9.7 %all_to_all.27 = s32[1,8,2]{2,0,1:T(1,128)S(1)} all-to-all(s32[1,8,2]{2,0,1:T(1,128)S(1)} %bitcast.86), channel_id=1, replica_groups=mesh['row'=4,'col'=8] {'col'}, dimensions={1} | all-to-all | bytes 128 | tf_op jit(solution)/shard_map/all_to_all | solution.py:50
  11.7 3.3 %all-to-all-start.2 = ((f32[1,8,256]{2,0,1:T(1,128)}), f32[1,8,256]{2,0,1:T(1,128)S(1)}, u32[]{:S(2)}, u32[]{:S(2)}) async-start(f32[1,8,256]{2,0,1:T(1,128)} %bitcast.87), calls=%async_computation.2 | async-start | bytes 16384 | tf_op jit(solution)/shard_map/all_to_all | solution.py:49
  15.1 0.8 %copy.28 = s32[16,8]{1,0:T(8,128)S(1)} copy(s32[16,8]{0,1:T(8,128)} %param.9) | data formatting | bytes 1024 | tf_op jit(solution)/shard_map/while | solution.py:42
  15.8 0.7 %reduce.9 = s32[8,2]{1,0:T(8,128)S(1)} reduce(s32[1,8,2]{2,0,1:T(1,128)S(1)} %all_to_all.27, s32[]{:T(128)} %broadcast.80), dimensions={0}, to_apply=%all_to_all.21.reduce_sub_computation.5 | reduce | bytes 132 | tf_op jit(solution)/shard_map/all_to_all | solution.py:50
  16.5 0.1 lt.37
  16.6 0.1 lt.40
  16.7 3.0 %all-to-all-done.2 = f32[1,8,256]{2,0,1:T(1,128)S(1)} async-done(((f32[1,8,256]{2,0,1:T(1,128)}), f32[1,8,256]{2,0,1:T(1,128)S(1)}, u32[]{:S(2)}, u32[]{:S(2)}) %all-to-all-start.2) | async-done | bytes 8224 | tf_op jit(solution)/shard_map/all_to_all | solution.py:49
  19.7 3.3 %all-to-all-start = ((f32[3,8,256]{2,0,1:T(4,128)}), f32[3,8,256]{2,0,1:T(4,128)S(1)}, u32[]{:S(2)}, u32[]{:S(2)}) async-start(f32[3,8,256]{2,0,1:T(4,128)} %bitcast.83), calls=%async_computation | async-start | bytes 65536 | tf_op jit(solution)/shard_map/all_to_all | solution.py:48
  23.0 0.1 fusion.11
  23.1 4.7 %all-to-all-done = f32[3,8,256]{2,0,1:T(4,128)S(1)} async-done(((f32[3,8,256]{2,0,1:T(4,128)}), f32[3,8,256]{2,0,1:T(4,128)S(1)}, u32[]{:S(2)}, u32[]{:S(2)}) %all-to-all-start) | async-done | bytes 24608 | tf_op jit(solution)/shard_map/all_to_all | solution.py:48
  27.8 1.6 %collective-permute-start = (f32[16,4,128]{2,0,1:T(8,128)S(1)}, f32[16,4,128]{2,0,1:T(8,128)S(1)}, u32[]{:S(2)}, u32[]{:S(2)}) collective-permute-start(f32[16,4,128]{2,0,1:T(8,128)S(1)} %get-tuple-element.91), channel_id=1, source_target_pairs={{0,8},{8,16},{16,24},{24,0},{1,9},{9,17},{17,25},{25,1},{2,10},{10... | collective-permute-start | bytes 98312 | tf_op jit(solution)/shard_map/ppermute | solution.py:16
  29.5 2.2 %collective-permute-start.1 = (f32[16,4,128]{2,0,1:T(8,128)S(1)}, f32[16,4,128]{2,0,1:T(8,128)S(1)}, u32[]{:S(2)}, u32[]{:S(2)}) collective-permute-start(f32[16,4,128]{2,0,1:T(8,128)S(1)} %get-tuple-element.91), channel_id=1, source_target_pairs={{8,0},{16,8},{24,16},{0,24},{9,1},{17,9},{25,17},{1,25},{10,2},{18... | collective-permute-start | bytes 98312 | tf_op jit(solution)/shard_map/ppermute | solution.py:17
  31.7 0.1 fusion.12
  31.8 1.9 %collective-permute-done = f32[16,4,128]{2,0,1:T(8,128)S(1)} collective-permute-done((f32[16,4,128]{2,0,1:T(8,128)S(1)}, f32[16,4,128]{2,0,1:T(8,128)S(1)}, u32[]{:S(2)}, u32[]{:S(2)}) %collective-permute-start) | collective-permute-done | bytes 32800 | tf_op jit(solution)/shard_map/ppermute | solution.py:16
  33.7 0.0 collective-permute-done.1
  33.8 10.0 %while.10 = (s32[]{:T(128)}, f32[2,8,3,128]{3,1,0,2:T(8,128)S(1)}, s32[2,8,8]{2,1,0:T(8,128)S(1)}, f32[48,4,128]{2,1,0:T(4,128)S(1)}, f32[2,8,4,128]{3,1,0,2:T(8,128)S(1)}, /*index=5*/f32[2,8,128]{2,1,0:T(8,128)S(1)}, s32[]{:T(128)}) while((s32[]{:T(128)}, f32[2,8,3,128]{3,1,0,2:T(8,128)S(1)}, s32[2,8,8]{2,1,0:T(8,128)S(1)}, ...), condition=%wide.region_4.5_spmd, body=%wide.region_0.4_spmd.sunk | while | flops 17833152 | bytes 779869 | solution.py:42
  33.8 0.1 reshape.198
  33.9 0.7 %gather_fusion = f32[64,4,128]{2,1,0:T(4,128)S(1)} fusion(f32[48,4,128]{2,1,0:T(4,128)S(1)} %get-tuple-element.166, s32[1024]{0:T(1024)S(1)} %pad_clamp_fusion.2), kind=kCustom, calls=%fused_computation.clone.1 | custom fusion | bytes 262400 | tf_op jit(solution)/shard_map/while/body/eval_jaxpr/gather | solution.py:31
  34.6 0.1 fusion.17
  34.7 4.0 %fusion.18 = (f32[8,128]{1,0:T(8,128)S(1)}, f32[8,128]{1,0:T(8,128)S(1)}, f32[8,128]{1,0:T(8,128)S(1)}) fusion(f32[8,128]{1,0:T(8,128)S(1)} %get-tuple-element.139, f32[8,8,128]{2,1,0:T(8,128)S(1)} %bitcast.76, f32[8,128]{1,0:T(8,128)S(1)} %get-tuple-element.141, f32[8,8,128]{2,1,0:T(8,128)S(1)} %bitcast.77, f32[8,128]{1,0:T(8,128)S(1)} %get-tuple-element.143, ...), kind=kLoop, calls=%fused_computation.11.clone.1 | loop fusion | flops 17822720 | bytes 155648 | tf_op jit(solution)/shard_map/while/body/eval_jaxpr/reduce_sum | solution.py:37
  38.8 0.1 reshape.198
  38.9 0.7 %gather_fusion = f32[64,4,128]{2,1,0:T(4,128)S(1)} fusion(f32[48,4,128]{2,1,0:T(4,128)S(1)} %get-tuple-element.166, s32[1024]{0:T(1024)S(1)} %pad_clamp_fusion.2), kind=kCustom, calls=%fused_computation.clone.1 | custom fusion | bytes 262400 | tf_op jit(solution)/shard_map/while/body/eval_jaxpr/gather | solution.py:31
  39.6 0.1 fusion.17
  39.7 4.0 %fusion.18 = (f32[8,128]{1,0:T(8,128)S(1)}, f32[8,128]{1,0:T(8,128)S(1)}, f32[8,128]{1,0:T(8,128)S(1)}) fusion(f32[8,128]{1,0:T(8,128)S(1)} %get-tuple-element.139, f32[8,8,128]{2,1,0:T(8,128)S(1)} %bitcast.76, f32[8,128]{1,0:T(8,128)S(1)} %get-tuple-element.141, f32[8,8,128]{2,1,0:T(8,128)S(1)} %bitcast.77, f32[8,128]{1,0:T(8,128)S(1)} %get-tuple-element.143, ...), kind=kLoop, calls=%fused_computation.11.clone.1 | loop fusion | flops 17822720 | bytes 155648 | tf_op jit(solution)/shard_map/while/body/eval_jaxpr/reduce_sum | solution.py:37
  43.8 0.6 %copy.34 = f32[1,3,16,128]{3,1,2,0:T(4,128)} copy(f32[1,3,16,128]{3,2,1,0:T(8,128)S(1)} %bitcast.85) | data formatting | bytes 49152
  (18 shorter events, 0.2 us)
Async XLA Ops:
  11.7 8.0 %all-to-all-start.2 = ((f32[1,8,256]{2,0,1:T(1,128)}), f32[1,8,256]{2,0,1:T(1,128)S(1)}, u32[]{:S(2)}, u32[]{:S(2)}) async-start(f32[1,8,256]{2,0,1:T(1,128)} %bitcast.87), calls=%async_computation.2 | async-start | bytes 16384 | tf_op jit(solution)/shard_map/all_to_all | solution.py:49
  19.7 8.1 %all-to-all-start = ((f32[3,8,256]{2,0,1:T(4,128)}), f32[3,8,256]{2,0,1:T(4,128)S(1)}, u32[]{:S(2)}, u32[]{:S(2)}) async-start(f32[3,8,256]{2,0,1:T(4,128)} %bitcast.83), calls=%async_computation | async-start | bytes 65536 | tf_op jit(solution)/shard_map/all_to_all | solution.py:48
  27.8 5.9 %collective-permute-start = (f32[16,4,128]{2,0,1:T(8,128)S(1)}, f32[16,4,128]{2,0,1:T(8,128)S(1)}, u32[]{:S(2)}, u32[]{:S(2)}) collective-permute-start(f32[16,4,128]{2,0,1:T(8,128)S(1)} %get-tuple-element.91), channel_id=1, source_target_pairs={{0,8},{8,16},{16,24},{24,0},{1,9},{9,17},{17,25},{25,1},{2,10},{10... | collective-permute-start | bytes 98312 | tf_op jit(solution)/shard_map/ppermute | solution.py:16
  29.5 4.3 %collective-permute-start.1 = (f32[16,4,128]{2,0,1:T(8,128)S(1)}, f32[16,4,128]{2,0,1:T(8,128)S(1)}, u32[]{:S(2)}, u32[]{:S(2)}) collective-permute-start(f32[16,4,128]{2,0,1:T(8,128)S(1)} %get-tuple-element.91), channel_id=1, source_target_pairs={{8,0},{16,8},{24,16},{0,24},{9,1},{17,9},{25,17},{1,25},{10,2},{18... | collective-permute-start | bytes 98312 | tf_op jit(solution)/shard_map/ppermute | solution.py:17
where the time goes:
time: 44.8 us; the launch traced here: 44.4 us
  starting transfers between devices  10.6 us (24%)
  other arithmetic  10.4 us (23%)
  blocking collectives  9.68 us (22%)
  waiting for transfers between devices  9.65 us (22%)
  local copies, waits for them, and re-layouts  3.98 us (9%)
    all_to_all x1, blocking collectives, on_device(): lax.all_to_all(counts, 'col', split_axis=1, concat_axis=1, tiled=True)  9.68 us
    reduce_sum x2, other arithmetic, one_group(): pull_x = jnp.sum(weight * delta_x, axis=(1, 3))  8.08 us
    all_to_all x1, waiting for transfers between devices, on_device(): lax.all_to_all(positions, 'col', split_axis=1, concat_axis=1, tiled=True)  4.7 us
    all_to_all x1, starting transfers between devices, on_device(): lax.all_to_all(positions, 'col', split_axis=1, concat_axis=1, tiled=True)  3.34 us
    all_to_all x1, starting transfers between devices, on_device(): lax.all_to_all(masses, 'col', split_axis=1, concat_axis=1, tiled=True)  3.33 us
    all_to_all x1, waiting for transfers between devices, on_device(): lax.all_to_all(masses, 'col', split_axis=1, concat_axis=1, tiled=True)  3 us
    ppermute x1, starting transfers between devices, padded_2(): after = lax.ppermute(leading, axis, down)  2.25 us
    ppermute x1, waiting for transfers between devices, padded_2(): before = lax.ppermute(last, axis, up)  1.92 us
  transfers between devices with their start and end apart: 4, of which 3 were waited for; matrix products, arithmetic and copies ran while one was open for 4% of the time, Pallas kernels for 0%

commit v1 on v0

--- a/solution.py
+++ b/solution.py
@@ -45,7 +45,12 @@
 
 def on_device(positions, masses, counts, sources):
     coords, weights, livecount = (
-        lax.all_to_all(positions, "col", split_axis=1, concat_axis=1, tiled=True),
+        jnp.concatenate(
+            lax.all_to_all(
+                jnp.stack(jnp.split(positions, lax.axis_size("col"), axis=1)), "col", 0, 0
+            ),
+            axis=1,
+        ),
         lax.all_to_all(masses, "col", split_axis=1, concat_axis=1, tiled=True),
         lax.all_to_all(counts, "col", split_axis=1, concat_axis=1, tiled=True),
     )

time: 44.8 us -> 50.9 us (1.14)
  local copies, waits for them, and re-layouts: 3.98 us -> 14.8 us
  blocking collectives: 9.68 us -> 0 us
  starting transfers between devices: 10.6 us -> 16.6 us
  waiting for transfers between devices: 9.65 us -> 8.51 us
    all_to_all x1 -> x0, blocking collectives: 9.68 us -> none  [on_device(): lax.all_to_all(counts, 'col', split_axis=1, concat_axis=1, tiled=True)]
    unnamed x2 -> x9, local copies, waits for them, and re-layouts: 1.22 us -> 10.1 us
    all_to_all x1 -> x2, starting transfers between devices: 3.34 us -> 8.54 us  [the longest x1 5.2 us: on_device(): lax.all_to_all(counts, 'col', split_axis=1, concat_axis=1, tiled=True)]
    another operation x0 -> x2, local copies, waits for them, and re-layouts: none -> 1.28 us  [the longest x1 1.28 us: on_device(): jnp.stack(jnp.split(positions, lax.axis_size('col'), axis=1))]
    all_to_all x1, waiting for transfers between devices: 3 us -> 1.86 us  [on_device(): lax.all_to_all(masses, 'col', split_axis=1, concat_axis=1, tiled=True)]
    all_to_all x1, starting transfers between devices: 3.33 us -> 4.2 us  [on_device(): lax.all_to_all(masses, 'col', split_axis=1, concat_axis=1, tiled=True)]
    all_to_all x1, local copies, waits for them, and re-layouts: 0.08 us -> 0.68 us  [on_device(): lax.all_to_all(counts, 'col', split_axis=1, concat_axis=1, tiled=True)]
    all_to_all x1 -> x2, waiting for transfers between devices: 4.7 us -> 4.7 us  [the longest x1 4.7 us: on_device(): lax.all_to_all(jnp.stack(jnp.split(positions, lax.axis_size('col'), axis=...]
  transfers between devices with their start and end apart: 4 -> 5, of which waited for: 3 -> 3; matrix products, arithmetic and copies ran while one was open for 4% -> 24% of each run, Pallas kernels for 0% -> 0%
where the time goes in v1:
time: 50.9 us; the launch traced here: 50.3 us
  starting transfers between devices  16.6 us (33%)
  local copies, waits for them, and re-layouts  14.8 us (29%)
  other arithmetic  10.2 us (20%)
  waiting for transfers between devices  8.51 us (17%)
    unnamed x9, local copies, waits for them, and re-layouts  10.1 us
    reduce_sum x2, other arithmetic, one_group(): pull_x = jnp.sum(weight * delta_x, axis=(1, 3))  8 us
    all_to_all x1, starting transfers between devices, on_device(): lax.all_to_all(counts, 'col', split_axis=1, concat_axis=1, tiled=True)  5.2 us
    all_to_all x1, waiting for transfers between devices, on_device(): lax.all_to_all(jnp.stack(jnp.split(positions, lax.axis_size('col'), axis=...  4.7 us
    all_to_all x1, starting transfers between devices, on_device(): lax.all_to_all(masses, 'col', split_axis=1, concat_axis=1, tiled=True)  4.2 us
    all_to_all x1, starting transfers between devices, on_device(): lax.all_to_all(jnp.stack(jnp.split(positions, lax.axis_size('col'), axis=...  3.34 us
    ppermute x1, starting transfers between devices, padded_2(): after = lax.ppermute(leading, axis, down)  2.25 us
    ppermute x1, waiting for transfers between devices, padded_2(): before = lax.ppermute(last, axis, up)  1.92 us
  transfers between devices with their start and end apart: 5, of which 3 were waited for; matrix products, arithmetic and copies ran while one was open for 24% of the time, Pallas kernels for 0%

profile of v1, /device:TPU:0, one launch (start us, length us, event | category | flops | bytes accessed | tf_op | source)
XLA Modules:
  0.0 50.3 jit_solution(13343203345484556276)
XLA Ops:
  0.0 0.5 %broadcast.80 = s32[]{:T(128)} broadcast(s32[]{:T(128)} %copy.44), dimensions={} | broadcast | bytes 8 | tf_op args[2]
  0.5 1.3 %reduce.8 = s32[16]{0:T(128)S(1)} reduce(s32[1,16]{1,0:T(1,128)} %param.8, s32[]{:T(128)} %broadcast.80), dimensions={0}, to_apply=%param.8.reduce_sub_computation.3 | reduce | bytes 132 | tf_op args[2]
  1.8 0.7 %all_to_all.16 = s32[1,8,2]{2,1,0:T(8,128)} reshape(s32[16]{0:T(128)S(1)} %reduce.8) | data formatting | bytes 128 | tf_op jit(solution)/shard_map/all_to_all | solution.py:55
  2.5 5.2 %all-to-all-start.1 = ((s32[1,8,2]{2,0,1:T(1,128)}), s32[1,8,2]{2,0,1:T(1,128)S(1)}, u32[]{:S(2)}, u32[]{:S(2)}) async-start(s32[1,8,2]{2,0,1:T(1,128)} %bitcast.24), calls=%async_computation.1 | async-start | bytes 8192 | tf_op jit(solution)/shard_map/all_to_all | solution.py:55
  7.7 1.3 %constant_dynamic-update-slice_fusion.7 = f32[8,3,256]{2,1,0:T(4,128)} fusion(f32[3,2048]{1,0:T(4,128)} %param.6), kind=kLoop, calls=%fused_computation.37 | loop fusion | bytes 7168
  9.0 1.3 %constant_dynamic-update-slice_fusion.6 = f32[8,3,256]{2,1,0:T(4,128)} fusion(f32[8,3,256]{2,1,0:T(4,128)} %constant_dynamic-update-slice_fusion.7, f32[3,2048]{1,0:T(4,128)} %param.6), kind=kLoop, calls=%fused_computation.36 | loop fusion | bytes 8192
  10.3 1.3 %constant_dynamic-update-slice_fusion.5 = f32[8,3,256]{2,1,0:T(4,128)} fusion(f32[8,3,256]{2,1,0:T(4,128)} %constant_dynamic-update-slice_fusion.6, f32[3,2048]{1,0:T(4,128)} %param.6), kind=kLoop, calls=%fused_computation.35 | loop fusion | bytes 8192
  11.6 1.3 %constant_dynamic-update-slice_fusion.4 = f32[8,3,256]{2,1,0:T(4,128)} fusion(f32[8,3,256]{2,1,0:T(4,128)} %constant_dynamic-update-slice_fusion.5, f32[3,2048]{1,0:T(4,128)} %param.6), kind=kLoop, calls=%fused_computation.34 | loop fusion | bytes 8192
  12.8 1.3 %constant_dynamic-update-slice_fusion.3 = f32[8,3,256]{2,1,0:T(4,128)} fusion(f32[8,3,256]{2,1,0:T(4,128)} %constant_dynamic-update-slice_fusion.4, f32[3,2048]{1,0:T(4,128)} %param.6), kind=kLoop, calls=%fused_computation.33 | loop fusion | bytes 8192
  14.1 1.3 %constant_dynamic-update-slice_fusion.2 = f32[8,3,256]{2,1,0:T(4,128)} fusion(f32[8,3,256]{2,1,0:T(4,128)} %constant_dynamic-update-slice_fusion.3, f32[3,2048]{1,0:T(4,128)} %param.6), kind=kLoop, calls=%fused_computation.32 | loop fusion | bytes 8192
  15.4 1.3 %constant_dynamic-update-slice_fusion.1 = f32[8,3,256]{2,1,0:T(4,128)} fusion(f32[8,3,256]{2,1,0:T(4,128)} %constant_dynamic-update-slice_fusion.2, f32[3,2048]{1,0:T(4,128)} %param.6), kind=kLoop, calls=%fused_computation.31 | loop fusion | bytes 8192
  16.7 0.0 all-to-all-done.1
  16.7 4.2 %all-to-all-start.2 = ((f32[1,8,256]{2,0,1:T(1,128)}), f32[1,8,256]{2,0,1:T(1,128)S(1)}, u32[]{:S(2)}, u32[]{:S(2)}) async-start(f32[1,8,256]{2,0,1:T(1,128)} %bitcast.102), calls=%async_computation.2 | async-start | bytes 16384 | tf_op jit(solution)/shard_map/all_to_all | solution.py:54
  20.9 1.3 %constant_dynamic-update-slice_fusion = f32[8,3,256]{2,1,0:T(4,128)} fusion(f32[8,3,256]{2,1,0:T(4,128)} %constant_dynamic-update-slice_fusion.1, f32[3,2048]{1,0:T(4,128)} %param.6), kind=kLoop, calls=%fused_computation.30 | loop fusion | bytes 8192 | tf_op jit(solution)/shard_map/stack | solution.py:50
  22.2 0.8 %copy.22 = s32[16,8]{1,0:T(8,128)S(1)} copy(s32[16,8]{0,1:T(8,128)} %param.9) | data formatting | bytes 1024 | tf_op jit(solution)/shard_map/while | solution.py:42
  22.9 0.6 %reduce.9 = s32[8,2]{1,0:T(8,128)S(1)} reduce(s32[1,8,2]{2,0,1:T(1,128)S(1)} %all-to-all-done.1, s32[]{:T(128)} %broadcast.80), dimensions={0}, to_apply=%all_to_all.17.reduce_sub_computation.5 | reduce | bytes 132 | tf_op jit(solution)/shard_map/all_to_all | solution.py:55
  23.6 0.1 lt.37
  23.7 0.1 lt.40
  23.7 1.9 %all-to-all-done.2 = f32[1,8,256]{2,0,1:T(1,128)S(1)} async-done(((f32[1,8,256]{2,0,1:T(1,128)}), f32[1,8,256]{2,0,1:T(1,128)S(1)}, u32[]{:S(2)}, u32[]{:S(2)}) %all-to-all-start.2) | async-done | bytes 8224 | tf_op jit(solution)/shard_map/all_to_all | solution.py:54
  25.6 3.3 %all-to-all-start = ((f32[8,3,256]{2,1,0:T(4,128)}), f32[8,3,256]{2,1,0:T(4,128)S(1)}, u32[]{:S(2)}, u32[]{:S(2)}) async-start(f32[8,3,256]{2,1,0:T(4,128)} %constant_dynamic-update-slice_fusion), calls=%async_computation | async-start | bytes 65536 | tf_op jit(solution)/shard_map/all_to_all | solution.py:49
  28.9 0.1 fusion.11
  29.0 4.7 %all-to-all-done = f32[8,3,256]{2,1,0:T(4,128)S(1)} async-done(((f32[8,3,256]{2,1,0:T(4,128)}), f32[8,3,256]{2,1,0:T(4,128)S(1)}, u32[]{:S(2)}, u32[]{:S(2)}) %all-to-all-start) | async-done | bytes 24608 | tf_op jit(solution)/shard_map/all_to_all | solution.py:49
  33.7 1.6 %collective-permute-start = (f32[16,4,128]{2,0,1:T(8,128)S(1)}, f32[16,4,128]{2,0,1:T(8,128)S(1)}, u32[]{:S(2)}, u32[]{:S(2)}) collective-permute-start(f32[16,4,128]{2,0,1:T(8,128)S(1)} %get-tuple-element.91), channel_id=1, source_target_pairs={{0,8},{8,16},{16,24},{24,0},{1,9},{9,17},{17,25},{25,1},{2,10},{10... | collective-permute-start | bytes 98312 | tf_op jit(solution)/shard_map/ppermute | solution.py:16
  35.4 2.2 %collective-permute-start.1 = (f32[16,4,128]{2,0,1:T(8,128)S(1)}, f32[16,4,128]{2,0,1:T(8,128)S(1)}, u32[]{:S(2)}, u32[]{:S(2)}) collective-permute-start(f32[16,4,128]{2,0,1:T(8,128)S(1)} %get-tuple-element.91), channel_id=1, source_target_pairs={{8,0},{16,8},{24,16},{0,24},{9,1},{17,9},{25,17},{1,25},{10,2},{18... | collective-permute-start | bytes 98312 | tf_op jit(solution)/shard_map/ppermute | solution.py:17
  37.6 0.1 fusion.12
  37.7 1.9 %collective-permute-done = f32[16,4,128]{2,0,1:T(8,128)S(1)} collective-permute-done((f32[16,4,128]{2,0,1:T(8,128)S(1)}, f32[16,4,128]{2,0,1:T(8,128)S(1)}, u32[]{:S(2)}, u32[]{:S(2)}) %collective-permute-start) | collective-permute-done | bytes 32800 | tf_op jit(solution)/shard_map/ppermute | solution.py:16
  39.6 0.0 collective-permute-done.1
  39.7 9.9 %while.10 = (s32[]{:T(128)}, f32[2,8,3,128]{3,1,0,2:T(8,128)S(1)}, s32[2,8,8]{2,1,0:T(8,128)S(1)}, f32[48,4,128]{2,1,0:T(4,128)S(1)}, f32[2,8,4,128]{3,1,0,2:T(8,128)S(1)}, /*index=5*/f32[2,8,128]{2,1,0:T(8,128)S(1)}, s32[]{:T(128)}) while((s32[]{:T(128)}, f32[2,8,3,128]{3,1,0,2:T(8,128)S(1)}, s32[2,8,8]{2,1,0:T(8,128)S(1)}, ...), condition=%wide.region_4.5_spmd, body=%wide.region_0.4_spmd.sunk | while | flops 17833152 | bytes 779869 | solution.py:42
  39.7 0.1 reshape.195
  39.8 0.7 %gather_fusion = f32[64,4,128]{2,1,0:T(4,128)S(1)} fusion(f32[48,4,128]{2,1,0:T(4,128)S(1)} %get-tuple-element.166, s32[1024]{0:T(1024)S(1)} %pad_clamp_fusion.2), kind=kCustom, calls=%fused_computation.clone.1 | custom fusion | bytes 262400 | tf_op jit(solution)/shard_map/while/body/eval_jaxpr/gather | solution.py:31
  40.5 0.1 fusion.17
  40.6 4.0 %fusion.18 = (f32[8,128]{1,0:T(8,128)S(1)}, f32[8,128]{1,0:T(8,128)S(1)}, f32[8,128]{1,0:T(8,128)S(1)}) fusion(f32[8,128]{1,0:T(8,128)S(1)} %get-tuple-element.139, f32[8,8,128]{2,1,0:T(8,128)S(1)} %bitcast.92, f32[8,128]{1,0:T(8,128)S(1)} %get-tuple-element.141, f32[8,8,128]{2,1,0:T(8,128)S(1)} %bitcast.93, f32[8,128]{1,0:T(8,128)S(1)} %get-tuple-element.143, ...), kind=kLoop, calls=%fused_computation.11.clone.1 | loop fusion | flops 17822720 | bytes 155648 | tf_op jit(solution)/shard_map/while/body/eval_jaxpr/reduce_sum | solution.py:37
  44.7 0.1 reshape.195
  44.8 0.7 %gather_fusion = f32[64,4,128]{2,1,0:T(4,128)S(1)} fusion(f32[48,4,128]{2,1,0:T(4,128)S(1)} %get-tuple-element.166, s32[1024]{0:T(1024)S(1)} %pad_clamp_fusion.2), kind=kCustom, calls=%fused_computation.clone.1 | custom fusion | bytes 262400 | tf_op jit(solution)/shard_map/while/body/eval_jaxpr/gather | solution.py:31
  45.4 0.1 fusion.17
  45.6 4.0 %fusion.18 = (f32[8,128]{1,0:T(8,128)S(1)}, f32[8,128]{1,0:T(8,128)S(1)}, f32[8,128]{1,0:T(8,128)S(1)}) fusion(f32[8,128]{1,0:T(8,128)S(1)} %get-tuple-element.139, f32[8,8,128]{2,1,0:T(8,128)S(1)} %bitcast.92, f32[8,128]{1,0:T(8,128)S(1)} %get-tuple-element.141, f32[8,8,128]{2,1,0:T(8,128)S(1)} %bitcast.93, f32[8,128]{1,0:T(8,128)S(1)} %get-tuple-element.143, ...), kind=kLoop, calls=%fused_computation.11.clone.1 | loop fusion | flops 17822720 | bytes 155648 | tf_op jit(solution)/shard_map/while/body/eval_jaxpr/reduce_sum | solution.py:37
  49.6 0.6 %copy.28 = f32[1,3,16,128]{3,1,2,0:T(4,128)} copy(f32[1,3,16,128]{3,2,1,0:T(8,128)S(1)} %bitcast.101) | data formatting | bytes 49152
  (18 shorter events, 0.2 us)
Async XLA Ops:
  2.5 14.2 %all-to-all-start.1 = ((s32[1,8,2]{2,0,1:T(1,128)}), s32[1,8,2]{2,0,1:T(1,128)S(1)}, u32[]{:S(2)}, u32[]{:S(2)}) async-start(s32[1,8,2]{2,0,1:T(1,128)} %bitcast.24), calls=%async_computation.1 | async-start | bytes 8192 | tf_op jit(solution)/shard_map/all_to_all | solution.py:55
  16.7 8.9 %all-to-all-start.2 = ((f32[1,8,256]{2,0,1:T(1,128)}), f32[1,8,256]{2,0,1:T(1,128)S(1)}, u32[]{:S(2)}, u32[]{:S(2)}) async-start(f32[1,8,256]{2,0,1:T(1,128)} %bitcast.102), calls=%async_computation.2 | async-start | bytes 16384 | tf_op jit(solution)/shard_map/all_to_all | solution.py:54
  25.6 8.1 %all-to-all-start = ((f32[8,3,256]{2,1,0:T(4,128)}), f32[8,3,256]{2,1,0:T(4,128)S(1)}, u32[]{:S(2)}, u32[]{:S(2)}) async-start(f32[8,3,256]{2,1,0:T(4,128)} %constant_dynamic-update-slice_fusion), calls=%async_computation | async-start | bytes 65536 | tf_op jit(solution)/shard_map/all_to_all | solution.py:49
  33.7 5.9 %collective-permute-start = (f32[16,4,128]{2,0,1:T(8,128)S(1)}, f32[16,4,128]{2,0,1:T(8,128)S(1)}, u32[]{:S(2)}, u32[]{:S(2)}) collective-permute-start(f32[16,4,128]{2,0,1:T(8,128)S(1)} %get-tuple-element.91), channel_id=1, source_target_pairs={{0,8},{8,16},{16,24},{24,0},{1,9},{9,17},{17,25},{25,1},{2,10},{10... | collective-permute-start | bytes 98312 | tf_op jit(solution)/shard_map/ppermute | solution.py:16
  35.4 4.3 %collective-permute-start.1 = (f32[16,4,128]{2,0,1:T(8,128)S(1)}, f32[16,4,128]{2,0,1:T(8,128)S(1)}, u32[]{:S(2)}, u32[]{:S(2)}) collective-permute-start(f32[16,4,128]{2,0,1:T(8,128)S(1)} %get-tuple-element.91), channel_id=1, source_target_pairs={{8,0},{16,8},{24,16},{0,24},{9,1},{17,9},{25,17},{1,25},{10,2},{18... | collective-permute-start | bytes 98312 | tf_op jit(solution)/shard_map/ppermute | solution.py:17
